TPU v7x, 32 devices: a whole 2x2x4 slice. The times are simulated.
32 devices in a mesh: layer: 4 (over z), tok: 8 (over y, x, core).
Axes of the slice: x: 2, y: 2, z: 4, core: 2. Of those that a mesh axis runs over, the one named last changes fastest.
Arguments:
- acts: bfloat16 [4, 8192, 4096], P('layer', 'tok'), may hold values from -48 to 48
- probe_weight: bfloat16 [4, 4096, 512], P('layer'), may hold values from -0.09375 to 0.09375
- mix_table: int32 [16, 2], replicated, may hold values from 0 to 3
- mix_scale: float32 [16], replicated, may hold values from 0.1 to 0.4
- labels: int32 [8192], P('tok'), may hold values from 0 to 511
Outputs:
- probe_grad: float32 [4, 4096, 512], P('layer', 'tok')
All inputs are finite; a program needn't handle non-finite values.
Results may differ from a plain program's by a relative error of at most 0.0028.
Values may be sent and summed in bfloat16 or wider, within the bound.
A program may use at most 256 MiB of HBM per device.

v0:
```python
import math

import jax
import jax.numpy as jnp
from jax import lax
from jax.sharding import PartitionSpec as P


def loss_grad(partial_value, labels, pick_a, pick_b, mix_scale, norm):
    classes = partial_value.shape[2]
    best = lax.Precision.HIGHEST
    first = jnp.einsum("ql,lnc->qnc", pick_a, partial_value, precision=best)
    second = jnp.einsum("ql,lnc->qnc", pick_b, partial_value, precision=best)
    logits = jnp.sum(partial_value, axis=0) + jnp.einsum(
        "q,qnc->nc", mix_scale, first * second, precision=best
    )
    top = jnp.max(logits, axis=1, keepdims=True)
    expo = jnp.exp(logits - top)
    probs = expo / jnp.sum(expo, axis=1, keepdims=True)
    onehot = (labels[:, None] == jnp.arange(classes, dtype=jnp.int32)[None, :]).astype(jnp.float32)
    grad = (probs - onehot) * norm
    weighted_a = pick_a * mix_scale[:, None]
    weighted_b = pick_b * mix_scale[:, None]
    factor = jnp.einsum("ql,qnc->lnc", weighted_a, second, precision=best) + jnp.einsum(
        "ql,qnc->lnc", weighted_b, first, precision=best
    )
    return (grad[None] * (1.0 + factor)).astype(jnp.bfloat16)


def local(acts, probe_weight, mix_table, mix_scale, labels):
    layers_dev, block_rows, width = acts.shape
    groups = lax.axis_size("layer")
    layers = layers_dev * groups
    rows_each = block_rows // groups
    norm = 1.0 / math.sqrt(block_rows * lax.axis_size("tok"))
    span = jnp.arange(layers, dtype=jnp.int32)[None, :]
    pick_a = (mix_table[:, 0:1] == span).astype(jnp.float32)
    pick_b = (mix_table[:, 1:2] == span).astype(jnp.float32)
    partial_value = jnp.einsum(
        "ltd,ldc->ltc", acts, probe_weight, preferred_element_type=jnp.float32
    )
    arrived = lax.all_to_all(partial_value, "layer", split_axis=1, concat_axis=0, tiled=True)
    start = lax.axis_index("layer") * rows_each
    own_labels = lax.dynamic_slice_in_dim(labels, start, rows_each, 0)
    dpartial = loss_grad(arrived, own_labels, pick_a, pick_b, mix_scale, norm)
    returned = lax.all_to_all(dpartial, "layer", split_axis=0, concat_axis=1, tiled=True)
    summed = lax.psum_scatter(
        jnp.einsum("ltd,ltc->dlc", acts, returned, preferred_element_type=jnp.float32),
        "tok",
        scatter_dimension=0,
        tiled=True,
    )
    return summed.transpose(1, 0, 2)


def solution(mesh):
    in_specs = (P("layer", "tok", None), P("layer", None, None), P(), P(), P("tok"))
    out_specs = P("layer", "tok", None)
    return jax.shard_map(local, mesh=mesh, in_specs=in_specs, out_specs=out_specs, check_vma=False)
```

profile of v0, /device:TPU:0, one launch (start us, length us, event | category | flops | bytes accessed | tf_op | source)
XLA Modules:
  0.0 219.2 jit_solution(3958546251618266344)
XLA Ops:
  6.5 8.1 %fusion.14 = f32[1,1024,512]{2,1,0:T(8,128)S(1)} fusion(bf16[1,4096,512]{2,1,0:T(8,128)(2,1)} %param.6, bf16[1,1024,4096]{2,1,0:T(8,128)(2,1)} %param.5), kind=kOutput, calls=%fused_computation.13 | convolution fusion | flops 4294967296 | bytes 14680064 | tf_op jit(solution)/shard_map/ltd,ldc->ltc/dot_general | solution.py:39
  14.7 0.0 copy-start.3
  14.7 3.5 %copy.16 = f32[1,1024,512]{2,0,1:T(1,128)} copy(f32[1,1024,512]{2,1,0:T(8,128)S(1)} %fusion.14) | data formatting | bytes 4194304 | tf_op jit(solution)/shard_map/ltd,ldc->ltc/dot_general | solution.py:39
  18.2 6.3 %all-to-all-start = ((f32[1,1024,512]{2,0,1:T(1,128)}), f32[1,1024,512]{2,0,1:T(1,128)}, u32[]{:S(2)}, u32[]{:S(2)}) async-start(f32[1,1024,512]{2,0,1:T(1,128)} %copy.16), calls=%async_computation | async-start | bytes 4194304 | tf_op jit(solution)/shard_map/all_to_all | solution.py:42
  24.5 0.0 reduce-scatter.2.cloned.1.call-start
  24.5 0.8 dynamic_slice.3
  25.3 0.0 copy-done.3
  25.3 47.5 %all-to-all-done = f32[1,1024,512]{2,0,1:T(1,128)} async-done(((f32[1,1024,512]{2,0,1:T(1,128)}), f32[1,1024,512]{2,0,1:T(1,128)}, u32[]{:S(2)}, u32[]{:S(2)}) %all-to-all-start) | async-done | bytes 2097184 | tf_op jit(solution)/shard_map/all_to_all | solution.py:42
  72.8 1.8 copy.22
  74.6 5.0 %fusion.10 = f32[16,256,512]{2,0,1:T(8,128)S(1)} fusion(f32[4,256,512]{2,1,0:T(8,128)S(1)} %bitcast.53, s32[16]{0:T(128)S(1)} %get-tuple-element.6), kind=kOutput, calls=%fused_computation.9 | convolution fusion | flops 100663360 | bytes 10485824 | tf_op jit(solution)/shard_map/ql,lnc->qnc/dot_general | solution.py:13
  79.6 0.0 copy-start.2
  79.6 5.0 %fusion.12 = f32[16,256,512]{2,0,1:T(8,128)S(1)} fusion(f32[4,256,512]{2,1,0:T(8,128)S(1)} %bitcast.54, s32[16]{0:T(128)S(1)} %get-tuple-element.5), kind=kOutput, calls=%fused_computation.11 | convolution fusion | flops 100663360 | bytes 10485824 | tf_op jit(solution)/shard_map/ql,lnc->qnc/dot_general | solution.py:12
  84.6 0.0 copy-done.2
  84.6 0.0 copy-start
  84.6 5.5 %fusion.21 = f32[4,256,512]{2,0,1:T(4,128)} fusion(f32[16,256,512]{2,0,1:T(8,128)S(1)} %fusion.10, f32[16]{0:T(128)S(1)} %copy-done.2, s32[16]{0:T(128)S(1)} %get-tuple-element.5), kind=kOutput, calls=%fused_computation.20 | convolution fusion | flops 100663424 | bytes 10485888 | tf_op jit(solution)/shard_map/ql,qnc->lnc/dot_general | solution.py:24
  90.0 0.0 copy-done
  90.0 5.2 %fusion.4 = f32[1,256,512]{2,0,1:T(1,128)S(1)} fusion(f32[16,256,512]{2,0,1:T(8,128)S(1)} %fusion.12, f32[16,256,512]{2,0,1:T(8,128)S(1)} %fusion.10, f32[16]{0:T(128)S(1)} %copy-done.2), kind=kOutput, calls=%fused_computation.4 | convolution fusion | flops 27262976 | bytes 17301568 | tf_op jit(solution)/shard_map/q,qnc->nc/dot_general | solution.py:14
  95.2 0.2 reduce_sum.18
  95.5 0.0 copy-start.1
  95.5 0.1 fusion.40
  95.6 0.2 fusion.19
  95.8 0.0 slice-start
  95.8 0.2 subtract_multiply_fusion
  96.1 1.0 copy-done.1
  97.1 0.0 slice-start.1
  97.1 7.3 %multiply_convert_fusion = bf16[4,256,512]{2,0,1:T(4,128)(2,1)S(1)} fusion(f32[4,256,512]{2,0,1:T(4,128)S(1)} %copy-done.1, f32[16,256,512]{2,0,1:T(8,128)} %copy-done, f32[256,512]{1,0:T(8,128)S(1)} %subtract_multiply_fusion, f32[16]{0:T(128)S(1)} %copy-done.2, s32[16]{0:T(128)S(1)} %get-tuple-element.6), kind=kOutput, calls=%fused_computation.8 | convolution fusion | flops 102760576 | bytes 12058752 | tf_op jit(solution)/shard_map/ql,qnc->lnc/dot_general | solution.py:24
  104.4 0.2 copy.19
  104.6 27.7 %all_to_all.21 = bf16[4,256,512]{2,1,0:T(8,128)(2,1)S(1)} all-to-all(bf16[4,256,512]{2,1,0:T(8,128)(2,1)S(1)} %copy.19), channel_id=1, replica_groups=mesh['layer'=4,'tok'=8] {'layer'}, dimensions={0} | all-to-all | bytes 2097152 | tf_op jit(solution)/shard_map/all_to_all | solution.py:46
  132.3 0.0 slice-done
  132.3 0.0 slice-done.1
  132.3 6.9 %fusion.6 = f32[4096,1,512]{0,2,1:T(8,128)} fusion(bf16[1024,512]{1,0:T(8,128)(2,1)S(1)} %bitcast.58, bf16[1,1024,4096]{2,1,0:T(8,128)(2,1)S(1)} %bitcast.57), kind=kOutput, calls=%fused_computation.6 | convolution fusion | flops 4294967296 | bytes 17825792 | tf_op jit(solution)/shard_map/ltd,ltc->dlc/dot_general | solution.py:48
  139.2 0.0 reduce-scatter.2.cloned.1.call-update
  139.2 70.6 %reduce-scatter.2.cloned.1.call-done = f32[512,1,512]{0,2,1:T(8,128)} async-done(((f32[4096,1,512]{0,2,1:T(8,128)}), f32[512,1,512]{0,2,1:T(8,128)}) %reduce-scatter.2.cloned.1.call-update) | async-done | bytes 1048592 | tf_op jit(solution)/shard_map/reduce_scatter | solution.py:47
  209.8 2.5 %copy.20 = f32[1,512,512]{2,1,0:T(8,128)} copy(f32[1,512,512]{1,2,0:T(8,128)} %bitcast.59) | data formatting | bytes 2097152 | tf_op jit(solution)/shard_map/transpose | solution.py:53
  (2 shorter events, 0.0 us)
Async XLA Ops:
  14.7 10.6 %copy-start.3 = (s32[16,2]{0,1:T(2,128)S(1)}, s32[16,2]{0,1:T(2,128)}, u32[]{:S(2)}) copy-start(s32[16,2]{0,1:T(2,128)} %param.7) | copy-start | bytes 388
  18.2 54.6 %all-to-all-start = ((f32[1,1024,512]{2,0,1:T(1,128)}), f32[1,1024,512]{2,0,1:T(1,128)}, u32[]{:S(2)}, u32[]{:S(2)}) async-start(f32[1,1024,512]{2,0,1:T(1,128)} %copy.16), calls=%async_computation | async-start | bytes 4194304 | tf_op jit(solution)/shard_map/all_to_all | solution.py:42
  24.5 185.3 %reduce-scatter.2.cloned.1.call-start = ((), (), s32[]{:S(2)}) async-start(), calls=%async_computation.3 | async-start | bytes 9437184 | tf_op jit(solution)/shard_map/reduce_scatter | solution.py:47
  79.6 5.0 %copy-start.2 = (f32[16]{0:T(128)S(1)}, f32[16]{0:T(128)}, u32[]{:S(2)}) copy-start(f32[16]{0:T(128)} %param.8) | copy-start | bytes 196
  84.6 5.5 %copy-start = (f32[16,256,512]{2,0,1:T(8,128)}, f32[16,256,512]{2,0,1:T(8,128)S(1)}, u32[]{:S(2)}) copy-start(f32[16,256,512]{2,0,1:T(8,128)S(1)} %fusion.12) | copy-start | bytes 25165828
  95.5 1.6 copy-start.1
  95.8 36.5 %slice-start = ((s8[8388608]{0:T(1024)(128)(4,1)}), s8[4194304]{0:T(1024)(128)(4,1)S(1)}, s32[]{:S(2)}) async-start(s8[8388608]{0:T(1024)(128)(4,1)} %bitcast.56), calls=%async_computation.4 | async-start | bytes 8388608
  97.1 35.2 %slice-start.1 = ((s8[8388608]{0:T(1024)(128)(4,1)}), s8[4194304]{0:T(1024)(128)(4,1)S(1)}, s32[]{:S(2)}) async-start(s8[8388608]{0:T(1024)(128)(4,1)} %bitcast.56), calls=%async_computation.5 | async-start | bytes 8388608
Sparse Core Ops, SparseCore 0:
  139.3 70.4 reduce-scatter.1
where the time goes:
time: 220 us; the launch traced here: 219 us
  waiting for transfers between devices  118 us (54%)
  matrix products  42.9 us (20%)
  blocking collectives  27.7 us (13%)
  between operations  13.5 us (6%)
  local copies, waits for them, and re-layouts  9.71 us (4%)
  starting transfers between devices  6.35 us (3%)
    reduce_scatter x1, waiting for transfers between devices, local(): lax.psum_scatter(jnp.einsum('ltd,ltc->dlc', acts, returned, preferred_ele...  70.6 us
    all_to_all x1, waiting for transfers between devices, local(): lax.all_to_all(partial_value, 'layer', split_axis=1, concat_axis=0, tiled...  47.5 us
    all_to_all x1, blocking collectives, local(): lax.all_to_all(dpartial, 'layer', split_axis=0, concat_axis=1, tiled=True)  27.7 us
    dot_general x1, matrix products, local(): jnp.einsum('ltd,ldc->ltc', acts, probe_weight, preferred_element_type=jnp...  8.14 us
    dot_general x1, matrix products, loss_grad(): jnp.einsum('ql,qnc->lnc', weighted_b, first, precision=best)  7.31 us
    dot_general x1, matrix products, local(): jnp.einsum('ltd,ltc->dlc', acts, returned, preferred_element_type=jnp.flo...  6.9 us
    all_to_all x1, starting transfers between devices, local(): lax.all_to_all(partial_value, 'layer', split_axis=1, concat_axis=0, tiled...  6.35 us
    dot_general x1, matrix products, loss_grad(): jnp.einsum('ql,qnc->lnc', weighted_a, second, precision=best)  5.46 us
  transfers between devices with their start and end apart: 2, of which 2 were waited for; matrix products, arithmetic and copies ran while one was open for 0% of the time, Pallas kernels for 0%

commit v1 on v0

v1 whole, which is shorter than its diff:
```python
import functools
import math

import jax
import jax.numpy as jnp
from jax import lax
from jax.experimental import pallas as pl
from jax.experimental.pallas import tpu as pltpu
from jax.sharding import PartitionSpec as P

MESH = pl.DeviceIdType.MESH
WIRE = jnp.int16
STEPS = 32767.0
SUB = 64
LANES = 128


def flip(value, bit):
    return value + bit - 2 * bit * ((value // bit) % 2)


def kernel(dims, table, scale, labels, acts, weight, out, acts_v, w_v, wire, got, wire_step, got_step, ret, dp, far_acts, far_dp, acc, rs_out, rs_in,
           s_acts, s_w, f_send, f_recv, g_send, g_recv, b_send, b_recv, a_send, a_recv, d_send, d_recv, r_send, r_recv):
    layers, subs, chips, stages, rows, width, classes, norm = dims
    each = rows // layers
    block = width // (2 * chips)
    me = lax.axis_index("layer")
    tok = lax.axis_index("tok")
    core = tok % 2
    chip = tok // 2
    mate = tok + 1 - 2 * core

    def load_acts(s, l):
        return pltpu.make_async_copy(
            acts.at[0, pl.ds(l * each + s * SUB, SUB), :], acts_v.at[s, pl.ds(l * SUB, SUB), :], s_acts.at[s, l]
        )

    load_w = pltpu.make_async_copy(weight.at[0], w_v, s_w)
    for l in range(layers):
        load_acts(0, l).start()
    load_w.start()
    for s in range(1, subs):
        for l in range(layers):
            load_acts(s, l).start()

    bits = []
    for i in range(stages):
        low, high = 2 ** i, 2 ** (stages - 1 - i)
        bits.append(low + core * (high - low))

    def chip_of(mask):
        where = chip
        for i in range(stages):
            if mask & (1 << i):
                where = flip(where, bits[i])
        return where

    peers = [lax.rem(me + k, layers) for k in sorted(range(1, layers), key=lambda k: abs(k - layers // 2))]
    barrier = pltpu.get_barrier_semaphore()
    for peer in peers:
        pl.semaphore_signal(barrier, inc=1, device_id=(peer, tok), device_id_type=MESH)
    pl.semaphore_signal(barrier, inc=1, device_id=(me, mate), device_id_type=MESH)
    for i in range(stages):
        pl.semaphore_signal(barrier, inc=1, device_id=(me, flip(chip, bits[i]) * 2 + core), device_id_type=MESH)

    def pair_step(q, totals):
        a, b, c = table[q, 0], table[q, 1], scale[q]
        new = []
        at = 0
        for l in range(layers):
            for m in range(l, layers):
                one = jnp.where((a == l) & (b == m), c, 0.0) + jnp.where((a == m) & (b == l), c, 0.0)
                new.append(totals[at] + one)
                at += 1
        return tuple(new)

    flat = lax.fori_loop(0, table.shape[0], pair_step, (jnp.float32(0.0),) * (layers * (layers + 1) // 2))
    mix = [[None] * layers for _ in range(layers)]
    at = 0
    for l in range(layers):
        for m in range(l, layers):
            mix[l][m] = mix[m][l] = flat[at]
            at += 1

    pl.semaphore_wait(barrier, layers - 1 + 1 + stages)

    def fwd_copy(s, peer):
        return pltpu.make_async_remote_copy(
            src_ref=wire.at[s, peer], dst_ref=got.at[s, me], send_sem=f_send.at[s, peer], recv_sem=f_recv.at[s, me],
            device_id=(peer, tok), device_id_type=MESH)

    def fwd_arrival(s, peer):
        return pltpu.make_async_remote_copy(
            src_ref=wire.at[s, peer], dst_ref=got.at[s, peer], send_sem=f_send.at[s, peer], recv_sem=f_recv.at[s, peer],
            device_id=(peer, tok), device_id_type=MESH)

    def step_copy(s, peer):
        return pltpu.make_async_remote_copy(
            src_ref=wire_step.at[s, peer], dst_ref=got_step.at[s, me], send_sem=g_send.at[s, peer], recv_sem=g_recv.at[s, me],
            device_id=(peer, tok), device_id_type=MESH)

    def step_arrival(s, peer):
        return pltpu.make_async_remote_copy(
            src_ref=wire_step.at[s, peer], dst_ref=got_step.at[s, peer], send_sem=g_send.at[s, peer], recv_sem=g_recv.at[s, peer],
            device_id=(peer, tok), device_id_type=MESH)

    def ret_copy(s, peer):
        return pltpu.make_async_remote_copy(
            src_ref=ret.at[s, peer], dst_ref=dp.at[s, pl.ds(me * SUB, SUB), :], send_sem=b_send.at[s, peer], recv_sem=b_recv.at[s, me],
            device_id=(peer, tok), device_id_type=MESH)

    def ret_arrival(s, peer):
        return pltpu.make_async_remote_copy(
            src_ref=ret.at[s, peer], dst_ref=dp.at[s, pl.ds(peer * SUB, SUB), :], send_sem=b_send.at[s, peer], recv_sem=b_recv.at[s, peer],
            device_id=(peer, tok), device_id_type=MESH)

    def cols(c, of_core):
        return pl.ds(pl.multiple_of((c * 2 + of_core) * block, block), block)

    def acts_copy(s, c):
        return pltpu.make_async_remote_copy(
            src_ref=acts_v.at[s, :, cols(c, 1 - core)], dst_ref=far_acts.at[s, c], send_sem=a_send.at[s, c], recv_sem=a_recv.at[s, c],
            device_id=(me, mate), device_id_type=MESH)

    def dp_copy(s):
        return pltpu.make_async_remote_copy(
            src_ref=dp.at[s], dst_ref=far_dp.at[s], send_sem=d_send.at[s], recv_sem=d_recv.at[s],
            device_id=(me, mate), device_id_type=MESH)

    load_w.wait()
    lane = lax.broadcasted_iota(jnp.int32, (SUB, LANES), 1)
    row = lax.broadcasted_iota(jnp.int32, (SUB, LANES), 0)

    def forward(s, _):
        for l in range(layers):
            load_acts(s, l).wait()
        part = jnp.dot(acts_v[s], w_v[...], preferred_element_type=jnp.float32)
        for l in range(layers):
            here = part[l * SUB:(l + 1) * SUB]
            reach = jnp.maximum(jnp.max(jnp.abs(here), axis=1, keepdims=True), 1e-30)
            wire[s, l] = jnp.round(here * (STEPS / reach)).astype(jnp.int32).astype(WIRE)
            spread = jnp.where(lane == row, jnp.broadcast_to(reach * (1.0 / STEPS), (SUB, LANES)), 0.0)
            wire_step[s, l] = jnp.sum(spread, axis=0, keepdims=True)
        for peer in peers:
            step_copy(s, peer).start()
            fwd_copy(s, peer).start()
        for c in range(chips):
            acts_copy(s, c).start()
        got[s, me] = wire[s, me]
        got_step[s, me] = wire_step[s, me]
        return 0

    lax.fori_loop(0, subs, forward, 0)

    span = lax.broadcasted_iota(jnp.int32, (SUB, classes), 1).astype(jnp.float32)

    def score(s, _):
        for peer in peers:
            fwd_arrival(s, peer).wait_recv()
            step_arrival(s, peer).wait_recv()
        first = me * each + s * SUB


        def column(line, shift):
            picked = jnp.where(lane == row + shift, jnp.broadcast_to(line, (SUB, LANES)), 0.0)
            return jnp.sum(picked, axis=1, keepdims=True)

        label = column(labels[pl.ds(first // LANES, 1), :].astype(jnp.float32), first % LANES)
        values = [got[s, l].astype(jnp.int32).astype(jnp.float32) * column(got_step[s, l], 0) for l in range(layers)]
        factors = []
        logits = None
        for l in range(layers):
            total = values[0] * mix[l][0]
            for m in range(1, layers):
                total = total + values[m] * mix[l][m]
            term = values[l] * (1.0 + 0.5 * total)
            logits = term if logits is None else logits + term
            factors.append(1.0 + total)
        top = jnp.max(logits, axis=1, keepdims=True)
        expo = jnp.exp(logits - top)
        probs = expo * (1.0 / jnp.sum(expo, axis=1, keepdims=True))
        grad = (probs - jnp.where(span == label, 1.0, 0.0)) * norm
        for l in range(layers):
            ret[s, l] = (grad * factors[l]).astype(jnp.bfloat16)
        for peer in peers:
            ret_copy(s, peer).start()
        dp[s, pl.ds(me * SUB, SUB), :] = ret[s, me]
        return 0

    lax.fori_loop(0, subs, score, 0)

    def product(s, mask):
        c = chip_of(mask)
        dims_ = (((0,), (0,)), ((), ()))
        near = lax.dot_general(acts_v[s, :, cols(c, core)], dp[s], dims_, preferred_element_type=jnp.float32)
        far = lax.dot_general(far_acts[s, c], far_dp[s], dims_, preferred_element_type=jnp.float32)
        return near + far

    def arrive(s):
        for peer in peers:
            ret_arrival(s, peer).wait_recv()
        dp_copy(s).start()
        for c in range(chips):
            acts_copy(s, c).wait_recv()
        dp_copy(s).wait_recv()

    for mask in range(chips):
        acc[mask] = jnp.zeros((block, classes), jnp.float32)

    def backward(s, _):
        arrive(s)
        for mask in range(chips):
            acc[mask] += product(s, mask)
        return 0

    lax.fori_loop(0, subs - 1, backward, 0)

    def low_bit(mask):
        return (mask & -mask).bit_length() - 1 if mask else stages

    def rs_copy(mask):
        i = low_bit(mask)
        return pltpu.make_async_remote_copy(
            src_ref=rs_out.at[mask - 1], dst_ref=rs_in.at[mask - 1], send_sem=r_send.at[mask - 1], recv_sem=r_recv.at[mask - 1],
            device_id=(me, flip(chip, bits[i]) * 2 + core), device_id_type=MESH)

    last = subs - 1
    arrive(last)
    order = sorted(range(chips), key=lambda mask: (low_bit(mask), -mask))
    waiting = []
    for mask in order:
        total = acc[mask] + product(last, mask)
        if low_bit(mask) == 0:
            rs_out[mask - 1] = total.astype(jnp.bfloat16)
            rs_copy(mask).start()
        else:
            acc[mask] = total
            waiting.append(mask)
    for mask in waiting:
        total = acc[mask]
        for i in range(low_bit(mask)):
            other = mask + (1 << i)
            rs_copy(other).wait_recv()
            total = total + rs_in[other - 1].astype(jnp.float32)
        if mask:
            rs_out[mask - 1] = total.astype(jnp.bfloat16)
            rs_copy(mask).start()
        else:
            out[0] = total

    def finish(s, _):
        for peer in peers:
            fwd_copy(s, peer).wait_send()
            step_copy(s, peer).wait_send()
            ret_copy(s, peer).wait_send()
        for c in range(chips):
            acts_copy(s, c).wait_send()
        dp_copy(s).wait_send()
        return 0

    lax.fori_loop(0, subs, finish, 0)
    for mask in range(1, chips):
        rs_copy(mask).wait_send()


def local(groups, toks, acts, probe_weight, mix_table, mix_scale, labels):
    _, rows, width = acts.shape
    classes = probe_weight.shape[2]
    each = rows // groups
    subs = each // SUB
    chips = toks // 2
    stages = chips.bit_length() - 1
    block = width // toks
    norm = 1.0 / math.sqrt(rows * toks)
    dims = (groups, subs, chips, stages, rows, width, classes, norm)
    mixed = groups * SUB
    dma = pltpu.SemaphoreType.DMA
    bf16 = jnp.bfloat16
    vmem = pl.BlockSpec(memory_space=pltpu.VMEM)
    smem = pl.BlockSpec(memory_space=pltpu.SMEM)
    hbm = pl.BlockSpec(memory_space=pl.ANY)
    return pl.pallas_call(
        functools.partial(kernel, dims),
        out_shape=jax.ShapeDtypeStruct((1, block, classes), jnp.float32),
        in_specs=[smem, smem, vmem, hbm, hbm],
        out_specs=vmem,
        scratch_shapes=[
            pltpu.VMEM((subs, mixed, width), bf16),
            pltpu.VMEM((width, classes), bf16),
            pltpu.VMEM((subs, groups, SUB, classes), WIRE),
            pltpu.VMEM((subs, groups, SUB, classes), WIRE),
            pltpu.VMEM((subs, groups, 1, LANES), jnp.float32),
            pltpu.VMEM((subs, groups, 1, LANES), jnp.float32),
            pltpu.VMEM((subs, groups, SUB, classes), bf16),
            pltpu.VMEM((subs, mixed, classes), bf16),
            pltpu.VMEM((subs, chips, mixed, block), bf16),
            pltpu.VMEM((subs, mixed, classes), bf16),
            pltpu.VMEM((chips, block, classes), jnp.float32),
            pltpu.VMEM((chips - 1, block, classes), bf16),
            pltpu.VMEM((chips - 1, block, classes), bf16),
            dma((subs, groups)), dma,
            dma((subs, groups)), dma((subs, groups)),
            dma((subs, groups)), dma((subs, groups)),
            dma((subs, groups)), dma((subs, groups)),
            dma((subs, chips)), dma((subs, chips)),
            dma((subs,)), dma((subs,)),
            dma((chips - 1,)), dma((chips - 1,)),
        ],
        compiler_params=pltpu.CompilerParams(collective_id=0, has_side_effects=True, vmem_limit_bytes=60 * 1024 * 1024),
    )(mix_table, mix_scale, labels.reshape(rows // LANES, LANES), acts, probe_weight)


def solution(mesh):
    in_specs = (P("layer", "tok", None), P("layer", None, None), P(), P(), P("tok"))
    out_specs = P("layer", "tok", None)
    body = functools.partial(local, mesh.shape["layer"], mesh.shape["tok"])
    return jax.shard_map(body, mesh=mesh, in_specs=in_specs, out_specs=out_specs, check_vma=False)
```

time: 220 us -> 83.6 us (0.38)
  waiting for transfers between devices: 118 us -> 0 us
  Pallas kernels: 0 us -> 79.7 us
  matrix products: 42.9 us -> 0 us
  blocking collectives: 27.7 us -> 0 us
  between operations: 13.5 us -> 0.01 us
  starting transfers between devices: 6.35 us -> 0 us
  local copies, waits for them, and re-layouts: 9.71 us -> 3.62 us
    pallas_call x0 -> x1, Pallas kernels: none -> 79.7 us  [local(): pl.pallas_call(functools.partial(kernel, dims), out_shape=jax.ShapeDtypeS...]
    reduce_scatter x1 -> x0, waiting for transfers between devices: 70.6 us -> none  [local(): lax.psum_scatter(jnp.einsum('ltd,ltc->dlc', acts, returned, preferred_ele...]
    all_to_all x1 -> x0, waiting for transfers between devices: 47.5 us -> none  [local(): lax.all_to_all(partial_value, 'layer', split_axis=1, concat_axis=0, tiled...]
    dot_general x7 -> x0, matrix products: 42.9 us -> none  [the longest x1 8.14 us: local(): jnp.einsum('ltd,ldc->ltc', acts, probe_weight, preferred_element_type=jnp...]
    all_to_all x1 -> x0, blocking collectives: 27.7 us -> none  [local(): lax.all_to_all(dpartial, 'layer', split_axis=0, concat_axis=1, tiled=True)]
    all_to_all x1 -> x0, starting transfers between devices: 6.35 us -> none  [local(): lax.all_to_all(partial_value, 'layer', split_axis=1, concat_axis=0, tiled...]
    dot_general x1 -> x0, local copies, waits for them, and re-layouts: 3.46 us -> none  [local(): jnp.einsum('ltd,ldc->ltc', acts, probe_weight, preferred_element_type=jnp...]
    transpose x1 -> x0, local copies, waits for them, and re-layouts: 2.53 us -> none  [local(): return summed.transpose(1, 0, 2)]
  transfers between devices with their start and end apart: 2 -> 0, of which waited for: 2 -> 0; matrix products, arithmetic and copies ran while one was open for 0% -> 0% of each run, Pallas kernels for 0% -> 0%
where the time goes in v1:
time: 83.6 us; the launch traced here: 83.3 us
  Pallas kernels  79.7 us (95%)
  local copies, waits for them, and re-layouts  3.62 us (4%)
    pallas_call x1, Pallas kernels, local(): pl.pallas_call(functools.partial(kernel, dims), out_shape=jax.ShapeDtypeS...  79.7 us
    unnamed x2, local copies, waits for them, and re-layouts  3.62 us

profile of v1, /device:TPU:0, one launch (start us, length us, event | category | flops | bytes accessed | tf_op | source)
XLA Modules:
  0.0 83.3 jit_solution(15392176584898992505)
XLA Ops:
  0.0 1.4 %copy.6.table = s32[16,2]{1,0:T(8,128)} copy(s32[16,2]{0,1:T(2,128)} %param.7) | data formatting | bytes 256 | tf_op args[2]
  1.4 79.7 %shard_map.55 = f32[1,512,512]{2,1,0:T(8,128)} custom-call(s32[16,2]{1,0:T(8,128)} %copy.6.table, f32[16]{0:T(128)} %scale.1, s32[8,128]{1,0:T(8,128)} %bitcast.1, bf16[1,1024,4096]{2,1,0:T(8,128)(2,1)} %acts.1, bf16[1,4096,512]{2,1,0:T(8,128)(2,1)} %weight.1), custom_call_target="tpu_custom_call" | custom-call | tf_op jit(solution)/shard_map/pallas_call | solution.py:282
  81.1 2.3 %copy.8 = f32[1,512,512]{2,1,0:T(8,128)} copy(f32[1,512,512]{2,1,0:T(8,128)} %shard_map.55) | data formatting | bytes 2097152

commit v2 on v1

--- a/solution.py
+++ b/solution.py
@@ -12,6 +12,7 @@
 WIRE = jnp.int16
 STEPS = 32767.0
 SUB = 64
+SLABS = 4
 LANES = 128
 
 
@@ -20,7 +21,7 @@
 
 
 def kernel(dims, table, scale, labels, acts, weight, out, acts_v, w_v, wire, got, wire_step, got_step, ret, dp, far_acts, far_dp, acc, rs_out, rs_in,
-           s_acts, s_w, f_send, f_recv, g_send, g_recv, b_send, b_recv, a_send, a_recv, d_send, d_recv, r_send, r_recv):
+           s_acts, s_slab, s_w, f_send, f_recv, g_send, g_recv, b_send, b_recv, a_send, a_recv, d_send, d_recv, r_send, r_recv):
     layers, subs, chips, stages, rows, width, classes, norm = dims
     each = rows // layers
     block = width // (2 * chips)
@@ -35,13 +36,18 @@
             acts.at[0, pl.ds(l * each + s * SUB, SUB), :], acts_v.at[s, pl.ds(l * SUB, SUB), :], s_acts.at[s, l]
         )
 
-    load_w = pltpu.make_async_copy(weight.at[0], w_v, s_w)
-    for l in range(layers):
-        load_acts(0, l).start()
-    load_w.start()
-    for s in range(1, subs):
-        for l in range(layers):
-            load_acts(s, l).start()
+    deep = width // SLABS
+
+    def load_slab(k):
+        span_k = pl.ds(k * deep, deep)
+        parts = [pltpu.make_async_copy(
+            acts.at[0, pl.ds(l * each, SUB), span_k], acts_v.at[0, pl.ds(l * SUB, SUB), span_k], s_slab.at[k, l]
+        ) for l in range(layers)]
+        return parts + [pltpu.make_async_copy(weight.at[0, span_k, :], w_v.at[span_k, :], s_w.at[k])]
+
+    for k in range(SLABS):
+        for load in load_slab(k):
+            load.start()
 
     bits = []
     for i in range(stages):
@@ -55,7 +61,14 @@
                 where = flip(where, bits[i])
         return where
 
-    peers = [lax.rem(me + k, layers) for k in sorted(range(1, layers), key=lambda k: abs(k - layers // 2))]
+    def other_layer(k):
+        where = me
+        for i in range((layers - 1).bit_length()):
+            if k & (1 << i):
+                where = flip(where, 1 << i)
+        return where
+
+    peers = [other_layer(k) for k in range(layers - 1, 0, -1)]
     barrier = pltpu.get_barrier_semaphore()
     for peer in peers:
         pl.semaphore_signal(barrier, inc=1, device_id=(peer, tok), device_id_type=MESH)
@@ -64,7 +77,7 @@
         pl.semaphore_signal(barrier, inc=1, device_id=(me, flip(chip, bits[i]) * 2 + core), device_id_type=MESH)
 
     def pair_step(q, totals):
-        a, b, c = table[q, 0], table[q, 1], scale[q]
+        a, b, c = table[0, q], table[1, q], scale[q]
         new = []
         at = 0
         for l in range(layers):
@@ -74,7 +87,7 @@
                 at += 1
         return tuple(new)
 
-    flat = lax.fori_loop(0, table.shape[0], pair_step, (jnp.float32(0.0),) * (layers * (layers + 1) // 2))
+    flat = lax.fori_loop(0, table.shape[1], pair_step, (jnp.float32(0.0),) * (layers * (layers + 1) // 2))
     mix = [[None] * layers for _ in range(layers)]
     at = 0
     for l in range(layers):
@@ -122,19 +135,16 @@
             src_ref=acts_v.at[s, :, cols(c, 1 - core)], dst_ref=far_acts.at[s, c], send_sem=a_send.at[s, c], recv_sem=a_recv.at[s, c],
             device_id=(me, mate), device_id_type=MESH)
 
-    def dp_copy(s):
-        return pltpu.make_async_remote_copy(
-            src_ref=dp.at[s], dst_ref=far_dp.at[s], send_sem=d_send.at[s], recv_sem=d_recv.at[s],
+    def dp_copy(s, l):
+        piece = pl.ds(l * SUB, SUB)
+        return pltpu.make_async_remote_copy(
+            src_ref=dp.at[s, piece, :], dst_ref=far_dp.at[s, piece, :], send_sem=d_send.at[s, l], recv_sem=d_recv.at[s, l],
             device_id=(me, mate), device_id_type=MESH)
 
-    load_w.wait()
     lane = lax.broadcasted_iota(jnp.int32, (SUB, LANES), 1)
     row = lax.broadcasted_iota(jnp.int32, (SUB, LANES), 0)
 
-    def forward(s, _):
-        for l in range(layers):
-            load_acts(s, l).wait()
-        part = jnp.dot(acts_v[s], w_v[...], preferred_element_type=jnp.float32)
+    def send_logits(s, part):
         for l in range(layers):
             here = part[l * SUB:(l + 1) * SUB]
             reach = jnp.maximum(jnp.max(jnp.abs(here), axis=1, keepdims=True), 1e-30)
@@ -148,9 +158,27 @@
             acts_copy(s, c).start()
         got[s, me] = wire[s, me]
         got_step[s, me] = wire_step[s, me]
+
+    part = None
+    for k in range(SLABS):
+        for load in load_slab(k):
+            load.wait()
+        span_k = pl.ds(k * deep, deep)
+        term = jnp.dot(acts_v[0, :, span_k], w_v[span_k, :], preferred_element_type=jnp.float32)
+        part = term if part is None else part + term
+        if k == SLABS - 2:
+            for s in range(1, subs):
+                for l in range(layers):
+                    load_acts(s, l).start()
+    send_logits(0, part)
+
+    def forward(s, _):
+        for l in range(layers):
+            load_acts(s, l).wait()
+        send_logits(s, jnp.dot(acts_v[s], w_v[...], preferred_element_type=jnp.float32))
         return 0
 
-    lax.fori_loop(0, subs, forward, 0)
+    lax.fori_loop(1, subs, forward, 0)
 
     span = lax.broadcasted_iota(jnp.int32, (SUB, classes), 1).astype(jnp.float32)
 
@@ -185,24 +213,29 @@
         for peer in peers:
             ret_copy(s, peer).start()
         dp[s, pl.ds(me * SUB, SUB), :] = ret[s, me]
+        dp_copy(s, me).start()
         return 0
 
     lax.fori_loop(0, subs, score, 0)
 
-    def product(s, mask):
-        c = chip_of(mask)
-        dims_ = (((0,), (0,)), ((), ()))
-        near = lax.dot_general(acts_v[s, :, cols(c, core)], dp[s], dims_, preferred_element_type=jnp.float32)
-        far = lax.dot_general(far_acts[s, c], far_dp[s], dims_, preferred_element_type=jnp.float32)
-        return near + far
+    contract = (((0,), (0,)), ((), ()))
+
+    def near(s, mask):
+        return lax.dot_general(acts_v[s, :, cols(chip_of(mask), core)], dp[s], contract, preferred_element_type=jnp.float32)
+
+    def far(s, mask):
+        return lax.dot_general(far_acts[s, chip_of(mask)], far_dp[s], contract, preferred_element_type=jnp.float32)
 
     def arrive(s):
-        for peer in peers:
+        for peer in peers[::-1]:
             ret_arrival(s, peer).wait_recv()
-        dp_copy(s).start()
+            dp_copy(s, peer).start()
+
+    def arrive_far(s):
         for c in range(chips):
             acts_copy(s, c).wait_recv()
-        dp_copy(s).wait_recv()
+        for l in range(layers):
+            dp_copy(s, l).wait_recv()
 
     for mask in range(chips):
         acc[mask] = jnp.zeros((block, classes), jnp.float32)
@@ -210,7 +243,10 @@
     def backward(s, _):
         arrive(s)
         for mask in range(chips):
-            acc[mask] += product(s, mask)
+            acc[mask] += near(s, mask)
+        arrive_far(s)
+        for mask in range(chips):
+            acc[mask] += far(s, mask)
         return 0
 
     lax.fori_loop(0, subs - 1, backward, 0)
@@ -226,10 +262,13 @@
 
     last = subs - 1
     arrive(last)
+    for mask in range(chips):
+        acc[mask] += near(last, mask)
+    arrive_far(last)
     order = sorted(range(chips), key=lambda mask: (low_bit(mask), -mask))
     waiting = []
     for mask in order:
-        total = acc[mask] + product(last, mask)
+        total = acc[mask] + far(last, mask)
         if low_bit(mask) == 0:
             rs_out[mask - 1] = total.astype(jnp.bfloat16)
             rs_copy(mask).start()
@@ -255,7 +294,8 @@
             ret_copy(s, peer).wait_send()
         for c in range(chips):
             acts_copy(s, c).wait_send()
-        dp_copy(s).wait_send()
+        for l in range(layers):
+            dp_copy(s, l).wait_send()
         return 0
 
     lax.fori_loop(0, subs, finish, 0)
@@ -281,7 +321,7 @@
     hbm = pl.BlockSpec(memory_space=pl.ANY)
     return pl.pallas_call(
         functools.partial(kernel, dims),
-        out_shape=jax.ShapeDtypeStruct((1, block, classes), jnp.float32),
+        out_shape=pltpu.VMEM((1, block, classes), jnp.float32),
         in_specs=[smem, smem, vmem, hbm, hbm],
         out_specs=vmem,
         scratch_shapes=[
@@ -298,16 +338,16 @@
             pltpu.VMEM((chips, block, classes), jnp.float32),
             pltpu.VMEM((chips - 1, block, classes), bf16),
             pltpu.VMEM((chips - 1, block, classes), bf16),
-            dma((subs, groups)), dma,
+            dma((subs, groups)), dma((SLABS, groups)), dma((SLABS,)),
             dma((subs, groups)), dma((subs, groups)),
             dma((subs, groups)), dma((subs, groups)),
             dma((subs, groups)), dma((subs, groups)),
             dma((subs, chips)), dma((subs, chips)),
-            dma((subs,)), dma((subs,)),
+            dma((subs, groups)), dma((subs, groups)),
             dma((chips - 1,)), dma((chips - 1,)),
         ],
         compiler_params=pltpu.CompilerParams(collective_id=0, has_side_effects=True, vmem_limit_bytes=60 * 1024 * 1024),
-    )(mix_table, mix_scale, labels.reshape(rows // LANES, LANES), acts, probe_weight)
+    )(mix_table.T, mix_scale, labels.reshape(rows // LANES, LANES), acts, probe_weight)
 
 
 def solution(mesh):

time: 83.6 us -> 78.3 us (0.937)
  local copies, waits for them, and re-layouts: 3.62 us -> 0.97 us
  Pallas kernels: 79.7 us -> 77.1 us
    unnamed x2 -> x1, local copies, waits for them, and re-layouts: 3.62 us -> 0.97 us
    pallas_call x1, Pallas kernels: 79.7 us -> 77.1 us  [local(): pl.pallas_call(functools.partial(kernel, dims), out_shape=pltpu.VMEM((1,...]
where the time goes in v2:
time: 78.3 us; the launch traced here: 78.1 us
  Pallas kernels  77.1 us (98%)
  local copies, waits for them, and re-layouts  0.97 us (1%)
    pallas_call x1, Pallas kernels, local(): pl.pallas_call(functools.partial(kernel, dims), out_shape=pltpu.VMEM((1,...  77.1 us

profile of v2, /device:TPU:0, one launch (start us, length us, event | category | flops | bytes accessed | tf_op | source)
XLA Modules:
  0.0 78.1 jit_solution(16331801570446060188)
XLA Ops:
  0.0 77.1 %shard_map.55 = f32[1,512,512]{2,1,0:T(8,128)S(1)} custom-call(s32[2,16]{1,0:T(2,128)} %bitcast.3, f32[16]{0:T(128)} %scale.1, s32[8,128]{1,0:T(8,128)} %bitcast.2, bf16[1,1024,4096]{2,1,0:T(8,128)(2,1)} %acts.1, bf16[1,4096,512]{2,1,0:T(8,128)(2,1)} %weight.1), custom_call_target="tpu_custom_call" | custom-call | tf_op jit(solution)/shard_map/pallas_call | solution.py:322
  77.1 1.0 %copy.7 = f32[1,512,512]{2,1,0:T(8,128)} copy(f32[1,512,512]{2,1,0:T(8,128)S(1)} %shard_map.55) | data formatting | bytes 2097152
